TPU v7x, 32 devices: a whole 2x2x4 slice. The times are simulated.
32 devices in a mesh: ctx: 8 (over z, core), head: 4 (over y, x).
Axes of the slice: x: 2, y: 2, z: 4, core: 2. Of those that a mesh axis runs over, the one named last changes fastest.
Arguments:
- queries: bfloat16 [1024, 8192], P('ctx', 'head'), parts along dimension 1, may hold values from -17 to 17
- keys: bfloat16 [1024, 512], P('ctx', 'head'), parts along dimension 1, may hold values from -17 to 17
- values: bfloat16 [1024, 512], P('ctx', 'head'), parts along dimension 1, may hold values from -6 to 6
- block_position: int32 [8], P('ctx'), may hold values from 0 to 7, each once
Outputs:
- attended: bfloat16 [1024, 8192], P('ctx', 'head'), parts along dimension 1
There are 4 independent parts, one for each index of `head`. A program takes and returns all parts, laid end to end along the dimension named above; an argument that names none is the same for every part. Nothing has to cross between parts.
All inputs are finite; a program needn't handle non-finite values.
Results may differ from a plain program's by a relative error of at most 0.005.
Values may be sent and summed in bfloat16 or wider, within the bound.
No kernel may reach another device: no remote copies, remote signals or barrier semaphores. Data moves between devices by JAX's collectives and lax.ppermute only.
A program may use at most 128 MiB of HBM per device.

v0:
```python
import math
import jax
import jax.numpy as jnp
from jax import lax
from jax.sharding import PartitionSpec as P

HEAD_DIM = 128
QHEADS = 16
BLOCK = 128


def body(queries, keys, values, block_position):
    local_rows = queries.shape[0]
    places = lax.all_gather(block_position, "ctx", axis=0, tiled=True)
    myself = lax.axis_index("ctx")
    row_ids = myself * local_rows + jnp.arange(local_rows, dtype=jnp.int32)
    query_pos = jnp.take(places, row_ids // BLOCK) * BLOCK + row_ids % BLOCK
    latest = jnp.max(query_pos)
    query_heads = queries.reshape(local_rows, QHEADS, HEAD_DIM).transpose(1, 0, 2)
    scale = 1.0 / math.sqrt(HEAD_DIM)
    initial = (
        jnp.full((QHEADS, local_rows), -1e30, jnp.float32),
        jnp.zeros((QHEADS, local_rows), jnp.float32),
        jnp.zeros((QHEADS, local_rows, HEAD_DIM), jnp.float32),
    )
    key_piece = lax.all_gather(keys, "ctx", axis=0, tiled=True)
    value_piece = lax.all_gather(values, "ctx", axis=0, tiled=True)
    piece_rows = key_piece.shape[0]
    key_ids = jnp.arange(piece_rows, dtype=jnp.int32)
    key_pos = jnp.take(places, key_ids // BLOCK) * BLOCK + key_ids % BLOCK

    def attend(state_in):
        running_max, denominator, numerator = state_in
        scores = (
            jnp.einsum("htd,nd->htn", query_heads, key_piece, preferred_element_type=jnp.float32)
            * scale
        )
        visible = key_pos[None, None, :] <= query_pos[None, :, None]
        new_max = jnp.maximum(running_max, jnp.max(jnp.where(visible, scores, -1e30), axis=-1))
        weights = jnp.where(visible, jnp.exp(scores - new_max[..., None]), 0.0)
        denominator = jnp.sum(weights, axis=-1)
        numerator = jnp.einsum(
            "htn,nd->htd",
            weights.astype(jnp.bfloat16),
            value_piece,
            preferred_element_type=jnp.float32,
        )
        return (new_max, denominator, numerator)

    final = lax.cond(jnp.min(key_pos) > latest, lambda state_in: state_in, attend, initial)
    running_max, denominator, numerator = final
    output = (numerator / denominator[..., None]).astype(jnp.bfloat16)
    return output.transpose(1, 0, 2).reshape(local_rows, QHEADS * HEAD_DIM)


def solution(mesh):
    placed = (P("ctx", "head"), P("ctx", "head"), P("ctx", "head"), P("ctx"))
    return jax.shard_map(
        body, mesh=mesh, in_specs=placed, out_specs=P("ctx", "head"), check_vma=False
    )
```

profile of v0, /device:TPU:0, one launch (start us, length us, event | category | flops | bytes accessed | tf_op | source)
XLA Modules:
  0.0 63.8 jit_solution(7075929578409433718)
XLA Ops:
  0.7 1.2 %dynamic-slice = u32[1]{0:T(128)} dynamic-slice(u32[32]{0:T(128)} %constant.118, u32[]{:T(128)S(6)} %add.115), dynamic_slice_sizes={1} | dynamic-slice | bytes 12
  1.9 0.8 %dynamic-update-slice = s32[8]{0:T(128)S(1)} dynamic-update-slice(s32[8]{0:T(128)S(1)} %broadcast.303, s32[1]{0:T(128)S(6)} %copy.17, u32[]{:T(128)} %bitcast.2) | dynamic-update-slice | bytes 12
  2.7 10.6 %all-reduce = s32[8]{0:T(128)S(1)} all-reduce(s32[8]{0:T(128)S(1)} %dynamic-update-slice), channel_id=1, replica_groups=mesh['ctx'=8,'head'=4] {'ctx'}, use_global_device_ids=true, to_apply=%add | all-reduce | flops 8 | bytes 64
  13.3 0.7 %fusion.29 = (s32[1]{0:T(128)}, s32[1]{0:T(128)}, s32[1]{0:T(128)}, s32[1]{0:T(128)}, s32[1]{0:T(128)}, /*index=5*/s32[1]{0:T(128)}, s32[1]{0:T(128)}, s32[1]{0:T(128)}) fusion(s32[8]{0:T(128)S(1)} %all-reduce), kind=kLoop, calls=%fused_computation.69 | loop fusion | bytes 64 | tf_op jit(solution)/shard_map/jit(_take)/gather | solution.py:30
  14.0 5.7 %fusion.25 = (s32[]{:T(128)}, s32[128]{0:T(128)S(1)}) fusion(s32[]{:T(128)} %bitcast.10, s32[]{:T(128)} %bitcast.9, s32[]{:T(128)} %bitcast.8, s32[]{:T(128)} %bitcast.7, s32[]{:T(128)} %bitcast.6, s32[]{:T(128)} %bitcast.5, s32[]{:T(128)} %bitcast.4, s32[]{:T(128)} %bitcast.3, s32[]{:T(128)S(6)} %mul.15), kind=kLoop, calls=%fused_computation.67 | loop fusion | flops 8063 | bytes 552 | tf_op jit(solution)/shard_map/reduce_max | solution.py:18
  19.7 4.3 %compare_select_fusion.1 = s32[1024,1]{0,1:T(1,128)S(1)} fusion(s32[]{:T(128)} %bitcast.4, s32[]{:T(128)} %bitcast.5, s32[]{:T(128)} %bitcast.6, s32[]{:T(128)} %bitcast.7, s32[]{:T(128)} %bitcast.8, s32[]{:T(128)} %bitcast.10, s32[]{:T(128)} %bitcast.9), kind=kLoop, calls=%fused_computation.18 | loop fusion | flops 23552 | bytes 4124 | tf_op jit(solution)/shard_map/jit(_take)/gather | solution.py:30
  24.0 1.3 %fusion.27 = (s32[]{:T(128)}, s32[1024]{0:T(1024)S(1)}) fusion(pred[1024]{0:T(1024)(128)(4,1)S(1)} %compare_reduce_fusion, s32[1024]{0:T(1024)S(1)} %bitcast.45, s32[]{:T(128)} %bitcast.3), kind=kLoop, calls=%fused_computation.68 | loop fusion | flops 23551 | bytes 9224 | tf_op jit(solution)/shard_map/reduce_min | solution.py:50
  26.5 14.4 %all_gather.10 = bf16[1024,128]{1,0:T(8,128)(2,1)S(1)} all-gather(bf16[128,128]{1,0:T(8,128)(2,1)} %param.7), channel_id=1, replica_groups=mesh['ctx'=8,'head'=4] {'ctx'}, dimensions={0}, use_global_device_ids=true | all-gather | bytes 294912 | tf_op jit(solution)/shard_map/all_gather | solution.py:26
  40.9 14.4 %all_gather.11 = bf16[1024,128]{1,0:T(8,128)(2,1)S(1)} all-gather(bf16[128,128]{1,0:T(8,128)(2,1)} %param.8), channel_id=1, replica_groups=mesh['ctx'=8,'head'=4] {'ctx'}, dimensions={0}, use_global_device_ids=true | all-gather | bytes 294912 | tf_op jit(solution)/shard_map/all_gather | solution.py:27
  55.3 1.3 %copy.6 = bf16[128,2048]{0,1:T(8,128)(2,1)S(1)} copy(bf16[128,2048]{1,0:T(8,128)(2,1)} %param.6) | data formatting | bytes 1048576 | tf_op args[0]
  56.6 6.0 %conditional.1 = (f32[16,128]{1,0:T(8,128)S(1)}, f32[16,128,128]{2,1,0:T(8,128)S(1)}) conditional(s32[]{:T(128)} %convert_element_type.9, (s32[1024]{0:T(1024)S(1)}, s32[128]{0:T(128)S(1)}, bf16[16,128,128]{1,2,0:T(8,128)(2,1)S(1)}, bf16[1024,128]{1,0:T(8,128)(2,1)S(1)}, bf16[1024,128]{1,0:T(8,128)(2,1)S(1)}) %tuple.28, () %tuple.14), branch_computations={%region_2.5_spmd, %region_5.6_spmd} | conditional | flops 1096939520 | bytes 27841040 | solution.py:50
  56.6 0.1 broadcast_compare_fusion
  56.8 1.6 %select_reduce_fusion = (f32[16,128]{1,0:T(8,128)S(1)}, f32[16,128,1024]{2,1,0:T(8,128)S(1)}) fusion(pred[128,1024]{1,0:T(8,128)(4,1)S(1)} %broadcast_compare_fusion, bf16[16,128,128]{1,2,0:T(8,128)(2,1)S(1)} %get-tuple-element.26, bf16[1024,128]{1,0:T(8,128)(2,1)S(1)} %get-tuple-element.18), kind=kOutput, calls=%fused_computation.1 | convolution fusion | flops 543160320 | bytes 9314304 | tf_op jit(solution)/shard_map/cond/branch_0_fun/htd,nd->htn/dot_general | solution.py:35
  58.4 2.4 %fusion.1 = f32[16,128]{1,0:T(8,128)S(1)} fusion(f32[16,128,1024]{2,1,0:T(8,128)S(1)} %get-tuple-element.34, f32[16,128]{1,0:T(8,128)S(1)} %broadcast_maximum_fusion, pred[128,1024]{1,0:T(8,128)(4,1)S(1)} %broadcast_compare_fusion), kind=kLoop, calls=%fused_computation.3 | loop fusion | flops 8386560 | bytes 8536064 | tf_op jit(solution)/shard_map/cond/branch_0_fun/reduce_sum | solution.py:41
  60.8 1.8 %fusion.2 = f32[16,128,128]{2,1,0:T(8,128)S(1)} fusion(f32[16,128,1024]{2,1,0:T(8,128)S(1)} %get-tuple-element.34, f32[16,128]{1,0:T(8,128)S(1)} %broadcast_maximum_fusion, pred[128,1024]{1,0:T(8,128)(4,1)S(1)} %broadcast_compare_fusion, bf16[1024,128]{1,0:T(8,128)(2,1)S(1)} %get-tuple-element.19), kind=kOutput, calls=%fused_computation.4 | convolution fusion | flops 545259520 | bytes 9838592 | tf_op jit(solution)/shard_map/cond/branch_0_fun/htn,nd->htd/dot_general | solution.py:42
  62.7 1.1 %copy_bitcast_fusion = bf16[128,2048]{1,0:T(8,128)(2,1)} fusion(f32[16,128,128]{2,1,0:T(8,128)S(1)} %get-tuple-element.22, f32[16,128]{1,0:T(8,128)S(1)} %get-tuple-element.23), kind=kLoop, calls=%fused_computation.14 | loop fusion | flops 524288 | bytes 1581056 | tf_op jit(solution)/shard_map/reshape | solution.py:53
  (3 shorter events, 0.0 us)
where the time goes:
time: 64.2 us; the launch traced here: 63.8 us
  blocking collectives  39.4 us (61%)
  other arithmetic  15 us (23%)
  local copies, waits for them, and re-layouts  4 us (6%)
  matrix products  3.44 us (5%)
  between operations  1.94 us (3%)
    all_gather x1, blocking collectives, body(): key_piece = lax.all_gather(keys, 'ctx', axis=0, tiled=True)  14.4 us
    all_gather x1, blocking collectives, body(): value_piece = lax.all_gather(values, 'ctx', axis=0, tiled=True)  14.4 us
    unnamed x1, blocking collectives  10.6 us
    reduce_max x1, other arithmetic, body(): latest = jnp.max(query_pos)  5.67 us
    gather x2, other arithmetic, body(): key_pos = jnp.take(places, key_ids // BLOCK) * BLOCK + key_ids % BLOCK  4.32 us
    unnamed x4, local copies, waits for them, and re-layouts  3.31 us
    reduce_sum x1, other arithmetic, attend(): denominator = jnp.sum(weights, axis=-1)  2.41 us
    dot_general x1, matrix products, attend(): jnp.einsum('htn,nd->htd', weights.astype(jnp.bfloat16), value_piece, pref...  1.84 us

commit v1 on v0

--- a/solution.py
+++ b/solution.py
@@ -23,8 +23,14 @@
         jnp.zeros((QHEADS, local_rows), jnp.float32),
         jnp.zeros((QHEADS, local_rows, HEAD_DIM), jnp.float32),
     )
-    key_piece = lax.all_gather(keys, "ctx", axis=0, tiled=True)
-    value_piece = lax.all_gather(values, "ctx", axis=0, tiled=True)
+
+    def _clear_teams(message, t0):
+        outcome_arr = lax.all_gather(
+            jnp.concatenate([message, t0], axis=1), "ctx", axis=0, tiled=True
+        )
+        return jnp.split(outcome_arr, [message.shape[1]], axis=1)
+
+    key_piece, value_piece = _clear_teams(keys, values)
     piece_rows = key_piece.shape[0]
     key_ids = jnp.arange(piece_rows, dtype=jnp.int32)
     key_pos = jnp.take(places, key_ids // BLOCK) * BLOCK + key_ids % BLOCK

time: 64.2 us -> 51 us (0.79)
  blocking collectives: 39.4 us -> 25.5 us
  other arithmetic: 15 us -> 15.7 us
    all_gather x2 -> x1, blocking collectives: 28.8 us -> 14.8 us  [_clear_teams(): lax.all_gather(jnp.concatenate([message, t0], axis=1), 'ctx', axis=0, til...]
    concatenate x0 -> x1, other arithmetic: none -> 0.79 us  [_clear_teams(): jnp.concatenate([message, t0], axis=1)]
where the time goes in v1:
time: 51 us; the launch traced here: 50.6 us
  blocking collectives  25.5 us (50%)
  other arithmetic  15.7 us (31%)
  local copies, waits for them, and re-layouts  4 us (8%)
  matrix products  3.36 us (7%)
  between operations  1.94 us (4%)
    all_gather x1, blocking collectives, _clear_teams(): lax.all_gather(jnp.concatenate([message, t0], axis=1), 'ctx', axis=0, til...  14.8 us
    unnamed x1, blocking collectives  10.6 us
    reduce_max x1, other arithmetic, body(): latest = jnp.max(query_pos)  5.67 us
    gather x2, other arithmetic, body(): key_pos = jnp.take(places, key_ids // BLOCK) * BLOCK + key_ids % BLOCK  4.32 us
    unnamed x4, local copies, waits for them, and re-layouts  3.31 us
    reduce_sum x1, other arithmetic, attend(): denominator = jnp.sum(weights, axis=-1)  2.41 us
    dot_general x1, matrix products, attend(): jnp.einsum('htn,nd->htd', weights.astype(jnp.bfloat16), value_piece, pref...  1.76 us
    dot_general x1, matrix products, attend(): jnp.einsum('htd,nd->htn', query_heads, key_piece, preferred_element_type=...  1.61 us

profile of v1, /device:TPU:0, one launch (start us, length us, event | category | flops | bytes accessed | tf_op | source)
XLA Modules:
  0.0 50.6 jit_solution(2110458882428455873)
XLA Ops:
  0.7 1.2 %dynamic-slice = u32[1]{0:T(128)} dynamic-slice(u32[32]{0:T(128)} %constant.118, u32[]{:T(128)S(6)} %add.115), dynamic_slice_sizes={1} | dynamic-slice | bytes 12
  1.9 0.8 %dynamic-update-slice = s32[8]{0:T(128)S(1)} dynamic-update-slice(s32[8]{0:T(128)S(1)} %broadcast.303, s32[1]{0:T(128)S(6)} %copy.17, u32[]{:T(128)} %bitcast.2) | dynamic-update-slice | bytes 12
  2.7 10.6 %all-reduce = s32[8]{0:T(128)S(1)} all-reduce(s32[8]{0:T(128)S(1)} %dynamic-update-slice), channel_id=1, replica_groups=mesh['ctx'=8,'head'=4] {'ctx'}, use_global_device_ids=true, to_apply=%add | all-reduce | flops 8 | bytes 64
  13.3 0.7 %fusion.31 = (s32[1]{0:T(128)}, s32[1]{0:T(128)}, s32[1]{0:T(128)}, s32[1]{0:T(128)}, s32[1]{0:T(128)}, /*index=5*/s32[1]{0:T(128)}, s32[1]{0:T(128)}, s32[1]{0:T(128)}) fusion(s32[8]{0:T(128)S(1)} %all-reduce), kind=kLoop, calls=%fused_computation.72 | loop fusion | bytes 64 | tf_op jit(solution)/shard_map/jit(_take)/gather | solution.py:36
  14.0 5.7 %fusion.27 = (s32[]{:T(128)}, s32[128]{0:T(128)S(1)}) fusion(s32[]{:T(128)} %bitcast.10, s32[]{:T(128)} %bitcast.9, s32[]{:T(128)} %bitcast.8, s32[]{:T(128)} %bitcast.7, s32[]{:T(128)} %bitcast.6, s32[]{:T(128)} %bitcast.5, s32[]{:T(128)} %bitcast.4, s32[]{:T(128)} %bitcast.3, s32[]{:T(128)S(6)} %mul.15), kind=kLoop, calls=%fused_computation.70 | loop fusion | flops 8063 | bytes 552 | tf_op jit(solution)/shard_map/reduce_max | solution.py:18
  19.7 4.3 %compare_select_fusion.1 = s32[1024,1]{0,1:T(1,128)S(1)} fusion(s32[]{:T(128)} %bitcast.4, s32[]{:T(128)} %bitcast.5, s32[]{:T(128)} %bitcast.6, s32[]{:T(128)} %bitcast.7, s32[]{:T(128)} %bitcast.8, s32[]{:T(128)} %bitcast.10, s32[]{:T(128)} %bitcast.9), kind=kLoop, calls=%fused_computation.21 | loop fusion | flops 23552 | bytes 4124 | tf_op jit(solution)/shard_map/jit(_take)/gather | solution.py:36
  24.0 1.3 %fusion.29 = (s32[]{:T(128)}, s32[1024]{0:T(1024)S(1)}) fusion(pred[1024]{0:T(1024)(128)(4,1)S(1)} %compare_reduce_fusion, s32[1024]{0:T(1024)S(1)} %bitcast.45, s32[]{:T(128)} %bitcast.3), kind=kLoop, calls=%fused_computation.71 | loop fusion | flops 23551 | bytes 9224 | tf_op jit(solution)/shard_map/reduce_min | solution.py:56
  26.5 0.8 %pad_maximum_fusion = bf16[128,256]{1,0:T(8,128)(2,1)S(1)} fusion(bf16[128,128]{1,0:T(8,128)(2,1)} %param.8, bf16[128,128]{1,0:T(8,128)(2,1)} %param.7), kind=kLoop, calls=%fused_computation.18 | loop fusion | flops 131072 | bytes 131072 | tf_op jit(solution)/shard_map/concatenate | solution.py:29
  27.3 14.8 %all_gather.7 = bf16[1024,256]{1,0:T(8,128)(2,1)S(1)} all-gather(bf16[128,256]{1,0:T(8,128)(2,1)S(1)} %pad_maximum_fusion), channel_id=1, replica_groups=mesh['ctx'=8,'head'=4] {'ctx'}, dimensions={0}, use_global_device_ids=true | all-gather | bytes 589824 | tf_op jit(solution)/shard_map/all_gather | solution.py:28
  42.1 1.3 %copy.6 = bf16[128,2048]{0,1:T(8,128)(2,1)S(1)} copy(bf16[128,2048]{1,0:T(8,128)(2,1)} %param.6) | data formatting | bytes 1048576 | tf_op args[0]
  43.5 6.0 %conditional.1 = (f32[16,128]{1,0:T(8,128)S(1)}, f32[16,128,128]{2,1,0:T(8,128)S(1)}) conditional(s32[]{:T(128)} %convert_element_type.9, (s32[1024]{0:T(1024)S(1)}, s32[128]{0:T(128)S(1)}, bf16[1024,256]{1,0:T(8,128)(2,1)S(1)}, bf16[16,128,128]{1,2,0:T(8,128)(2,1)S(1)}) %tuple.28, () %tuple.14), branch_computations={%region_2.5_spmd, %region_5.6_spmd} | conditional | flops 1096939520 | bytes 27841040 | solution.py:56
  43.5 0.1 broadcast_compare_fusion
  43.6 1.6 %select_reduce_fusion = (f32[16,128]{1,0:T(8,128)S(1)}, f32[16,128,1024]{2,1,0:T(8,128)S(1)}) fusion(pred[128,1024]{1,0:T(8,128)(4,1)S(1)} %broadcast_compare_fusion, bf16[16,128,128]{1,2,0:T(8,128)(2,1)S(1)} %get-tuple-element.27, bf16[1024,256]{1,0:T(8,128)(2,1)S(1)} %get-tuple-element.19), kind=kOutput, calls=%fused_computation.1 | convolution fusion | flops 543160320 | bytes 9314304 | tf_op jit(solution)/shard_map/cond/branch_0_fun/htd,nd->htn/dot_general | solution.py:41
  45.2 2.4 %fusion.1 = f32[16,128]{1,0:T(8,128)S(1)} fusion(f32[16,128,1024]{2,1,0:T(8,128)S(1)} %get-tuple-element.33, f32[16,128]{1,0:T(8,128)S(1)} %broadcast_maximum_fusion, pred[128,1024]{1,0:T(8,128)(4,1)S(1)} %broadcast_compare_fusion), kind=kLoop, calls=%fused_computation.3 | loop fusion | flops 8386560 | bytes 8536064 | tf_op jit(solution)/shard_map/cond/branch_0_fun/reduce_sum | solution.py:47
  47.7 1.8 %fusion.2 = f32[16,128,128]{2,1,0:T(8,128)S(1)} fusion(f32[16,128,1024]{2,1,0:T(8,128)S(1)} %get-tuple-element.33, f32[16,128]{1,0:T(8,128)S(1)} %broadcast_maximum_fusion, pred[128,1024]{1,0:T(8,128)(4,1)S(1)} %broadcast_compare_fusion, bf16[1024,256]{1,0:T(8,128)(2,1)S(1)} %get-tuple-element.19), kind=kOutput, calls=%fused_computation.4 | convolution fusion | flops 545259520 | bytes 9838592 | tf_op jit(solution)/shard_map/cond/branch_0_fun/htn,nd->htd/dot_general | solution.py:48
  49.4 1.1 %copy_bitcast_fusion = bf16[128,2048]{1,0:T(8,128)(2,1)} fusion(f32[16,128,128]{2,1,0:T(8,128)S(1)} %get-tuple-element.22, f32[16,128]{1,0:T(8,128)S(1)} %get-tuple-element.23), kind=kLoop, calls=%fused_computation.16 | loop fusion | flops 524288 | bytes 1581056 | tf_op jit(solution)/shard_map/reshape | solution.py:59
  (3 shorter events, 0.0 us)
